TPU v7x, 32 devices: a whole 2x2x4 slice. The times are simulated.
32 devices in a mesh: parts: 2 (over y), blk: 4 (over z), grp: 4 (over x, core).
Axes of the slice: x: 2, y: 2, z: 4, core: 2. Of those that a mesh axis runs over, the one named last changes fastest.
Arguments:
- factors: float32 [64, 4096], P(None, ('parts', 'blk', 'grp')), parts along dimension 1, may hold values from -1 to 1
- tangent: float32 [64, 4096], P(None, ('parts', 'blk', 'grp')), parts along dimension 1, may hold values from -15 to 15
- counts: int32 [4096, 2048], P(('parts', 'blk', 'grp')), parts along dimension 0, may hold values from 0 to 4, as said below
Outputs:
- hess_vec: float32 [64, 4096], P(None, ('parts', 'blk', 'grp')), parts along dimension 1
- residual: float32 [64, 4096], P(None, ('parts', 'blk', 'grp')), parts along dimension 1
- inner: float32 [4], P('parts'), parts along dimension 0
There are 2 independent parts, one for each index of `parts`. A program takes and returns all parts, laid end to end along the dimension named above; each array names one. Nothing has to cross between parts.
Inputs may be any that keep to these rules, and one draw needn't show every extreme that they name: counts is symmetric.
All inputs are finite; a program needn't handle non-finite values.
Results may differ from a plain program's by a relative error of at most 0.0003.
Values sent between devices are 32-bit elements; how exact they have to be, the bound alone decides.
A program may use at most 128 MiB of HBM per device.

v0:
```python
import jax
import jax.numpy as jnp
from jax import lax
from jax.sharding import PartitionSpec as P


def local(factors, tangent, counts):
    rows = counts.shape[0]
    nodes = counts.shape[1]
    scale = 1.0 / jnp.sqrt(jnp.float32(nodes))
    highest = lax.Precision.HIGHEST
    contract = (((0,), (0,)), ((), ()))
    right = (((1,), (1,)), ((), ()))
    row_start = (lax.axis_index("blk") * lax.axis_size("grp") + lax.axis_index("grp")) * rows
    row_ids = row_start + jnp.arange(rows, dtype=jnp.int32)[:, None]
    group_u, group_v = (
        lax.all_gather(factors, "grp", axis=1, tiled=True),
        lax.all_gather(tangent, "grp", axis=1, tiled=True),
    )
    piece_u = lax.all_gather(group_u, "blk", axis=1, tiled=True)
    piece_v = lax.all_gather(group_v, "blk", axis=1, tiled=True)
    width = piece_u.shape[1]
    eta = lax.dot_general(factors, piece_u, contract, precision=highest)
    deta = lax.dot_general(factors, piece_v, contract, precision=highest) + lax.dot_general(
        tangent, piece_u, contract, precision=highest
    )
    col_ids = jnp.arange(width, dtype=jnp.int32)[None, :]
    keep = row_ids != col_ids
    rate = jnp.where(keep, jnp.exp(eta), jnp.float32(0.0))
    weight = rate * deta
    tile_counts = counts.astype(jnp.float32)
    slack = jnp.where(keep, tile_counts - rate, jnp.float32(0.0))
    hess_acc = lax.dot_general(piece_u, weight, right, precision=highest)
    resid_acc = lax.dot_general(piece_u, slack - weight, right, precision=highest)
    hess_acc, resid_acc = (hess_acc, resid_acc)
    hess_vec = hess_acc * scale
    residual = resid_acc * scale
    sum_sq, sum_curv = lax.psum(
        (jnp.sum(residual * residual), jnp.sum(tangent * hess_vec)), ("blk", "grp")
    )
    inner = jnp.stack([sum_sq, sum_curv])
    return (hess_vec, residual, inner)


def solution(mesh):
    return jax.shard_map(
        local,
        mesh=mesh,
        in_specs=(
            P(None, ("parts", "blk", "grp")),
            P(None, ("parts", "blk", "grp")),
            P(("parts", "blk", "grp"), None),
        ),
        out_specs=(P(None, ("parts", "blk", "grp")), P(None, ("parts", "blk", "grp")), P("parts")),
        check_vma=False,
    )
```

profile of v0, /device:TPU:0, one launch (start us, length us, event | category | flops | bytes accessed | tf_op | source)
XLA Modules:
  0.0 85.9 jit_solution(17943244656120877728)
XLA Ops:
  0.6 0.0 copy-start.1
  0.7 6.7 %all_gather.12 = f32[64,512]{1,0:T(8,128)S(1)} all-gather(f32[64,128]{1,0:T(8,128)} %param.3), channel_id=1, replica_groups=mesh['parts'=2,'blk'=4,'grp'=4] {'grp'}, dimensions={1}, use_global_device_ids=true | all-gather | bytes 163840 | tf_op jit(solution)/shard_map/all_gather | solution.py:17
  7.4 0.0 copy-done.1
  7.4 5.6 %all_gather.14 = f32[64,512]{1,0:T(8,128)S(1)} all-gather(f32[64,128]{1,0:T(8,128)S(1)} %copy-done.1), channel_id=1, replica_groups=mesh['parts'=2,'blk'=4,'grp'=4] {'grp'}, dimensions={1}, use_global_device_ids=true | all-gather | bytes 163840 | tf_op jit(solution)/shard_map/all_gather | solution.py:18
  12.9 16.6 %all_gather.13 = f32[64,2048]{1,0:T(8,128)S(1)} all-gather(f32[64,512]{1,0:T(8,128)S(1)} %all_gather.12), channel_id=1, replica_groups=mesh['parts'=2,'blk'=4,'grp'=4] {'blk'}, dimensions={1}, use_global_device_ids=true | all-gather | bytes 655360 | tf_op jit(solution)/shard_map/all_gather | solution.py:20
  29.5 0.0 copy-start.2
  29.5 16.0 %all_gather.15 = f32[64,2048]{1,0:T(8,128)S(1)} all-gather(f32[64,512]{1,0:T(8,128)S(1)} %all_gather.14), channel_id=1, replica_groups=mesh['parts'=2,'blk'=4,'grp'=4] {'blk'}, dimensions={1}, use_global_device_ids=true | all-gather | bytes 655360 | tf_op jit(solution)/shard_map/all_gather | solution.py:21
  45.5 0.0 copy-done.2
  45.5 1.0 %fusion.11 = f32[128,2048]{1,0:T(8,128)S(1)} fusion(f32[64,128]{1,0:T(8,128)S(1)} %copy-done.2, f32[64,2048]{1,0:T(8,128)S(1)} %all_gather.15), kind=kOutput, calls=%fused_computation.20 | convolution fusion | flops 201326592 | bytes 1605632 | tf_op jit(solution)/shard_map/dot_general | solution.py:24
  46.6 1.1 %fusion.1 = f32[128,2048]{1,0:T(8,128)S(1)} fusion(f32[64,128]{1,0:T(8,128)S(1)} %copy-done.2, f32[64,2048]{1,0:T(8,128)S(1)} %all_gather.13, s32[128]{0:T(128)S(1)} %iota_add_fusion), kind=kOutput, calls=%fused_computation.3 | convolution fusion | flops 201850880 | bytes 1606144 | tf_op jit(solution)/shard_map/dot_general | solution.py:23
  47.7 0.0 copy-start
  47.7 1.1 %fusion = f32[128,2048]{1,0:T(8,128)S(1)} fusion(f32[128,2048]{1,0:T(8,128)S(1)} %fusion.1, f32[128,2048]{1,0:T(8,128)S(1)} %fusion.11, f32[64,128]{1,0:T(8,128)S(1)} %copy-done.1, f32[64,2048]{1,0:T(8,128)S(1)} %all_gather.13), kind=kOutput, calls=%fused_computation.1 | convolution fusion | flops 201850880 | bytes 3702784 | tf_op jit(solution)/shard_map/dot_general | solution.py:24
  48.8 0.2 copy-done
  48.9 2.7 %multiply_reduce_fusion.1 = (f32[]{:T(128)}, f32[64,128]{1,0:T(8,128)}) fusion(f32[64,2048]{1,0:T(8,128)S(1)} %all_gather.13, f32[128,2048]{1,0:T(8,128)S(1)} %fusion, f32[128,2048]{1,0:T(8,128)S(1)} %fusion.1, s32[128,2048]{1,0:T(8,128)S(1)} %copy-done, s32[128]{0:T(128)S(1)} %iota_add_fusion), kind=kOutput, calls=%fused_computation.16 | convolution fusion | flops 202661888 | bytes 3703300 | tf_op jit(solution)/shard_map/dot_general | solution.py:34
  51.6 2.4 %multiply_reduce_fusion = (f32[]{:T(128)}, f32[64,128]{1,0:T(8,128)}) fusion(f32[64,128]{1,0:T(8,128)S(1)} %copy-done.1, f32[128,2048]{1,0:T(8,128)S(1)} %fusion, f32[64,2048]{1,0:T(8,128)S(1)} %all_gather.13), kind=kOutput, calls=%fused_computation.15 | convolution fusion | flops 201351168 | bytes 1638404 | tf_op jit(solution)/shard_map/dot_general | solution.py:33
  54.0 30.1 %all-reduce = (f32[1]{0:T(128)}, f32[1]{0:T(128)}) all-reduce(f32[1]{0:T(128)} %bitcast.3, f32[1]{0:T(128)} %bitcast.2), channel_id=1, replica_groups=mesh['parts'=2,'blk'=4,'grp'=4] {'blk','grp'}, use_global_device_ids=true, to_apply=%region_3.4 | all-reduce | flops 2 | bytes 16 | tf_op jit(solution)/shard_map/psum | solution.py:38
  84.2 1.8 %pad_maximum_fusion = f32[2]{0:T(128)} fusion(f32[1]{0:T(128)} %get-tuple-element.3, f32[1]{0:T(128)} %get-tuple-element.4), kind=kLoop, calls=%fused_computation.17 | loop fusion | flops 2 | bytes 16 | tf_op jit(solution)/shard_map/stack | solution.py:41
  (1 shorter events, 0.0 us)
Async XLA Ops:
  0.6 6.7 %copy-start.1 = (f32[64,128]{1,0:T(8,128)S(1)}, f32[64,128]{1,0:T(8,128)}, u32[]{:S(2)}) copy-start(f32[64,128]{1,0:T(8,128)} %param.4) | copy-start | bytes 98308
  29.5 16.0 %copy-start.2 = (f32[64,128]{1,0:T(8,128)S(1)}, f32[64,128]{1,0:T(8,128)}, u32[]{:S(2)}) copy-start(f32[64,128]{1,0:T(8,128)} %param.3) | copy-start | bytes 98308
  47.7 1.2 %copy-start = (s32[128,2048]{1,0:T(8,128)S(1)}, s32[128,2048]{1,0:T(8,128)}, u32[]{:S(2)}) copy-start(s32[128,2048]{1,0:T(8,128)} %param.5) | copy-start | bytes 3145732
where the time goes:
time: 86.3 us; the launch traced here: 85.9 us
  blocking collectives  75 us (87%)
  matrix products  8.3 us (10%)
  other arithmetic  1.78 us (2%)
    psum x1, blocking collectives, local(): lax.psum((jnp.sum(residual * residual), jnp.sum(tangent * hess_vec)), ('b...  30.1 us
    all_gather x1, blocking collectives, local(): piece_u = lax.all_gather(group_u, 'blk', axis=1, tiled=True)  16.6 us
    all_gather x1, blocking collectives, local(): piece_v = lax.all_gather(group_v, 'blk', axis=1, tiled=True)  16 us
    all_gather x1, blocking collectives, local(): lax.all_gather(factors, 'grp', axis=1, tiled=True)  6.69 us
    all_gather x1, blocking collectives, local(): lax.all_gather(tangent, 'grp', axis=1, tiled=True)  5.58 us
    dot_general x1, matrix products, local(): lax.dot_general(piece_u, slack - weight, right, precision=highest)  2.69 us
    dot_general x1, matrix products, local(): hess_acc = lax.dot_general(piece_u, weight, right, precision=highest)  2.41 us
    another operation x1, other arithmetic, local(): inner = jnp.stack([sum_sq, sum_curv])  1.78 us

commit v1 on v0

--- a/solution.py
+++ b/solution.py
@@ -17,8 +17,11 @@
         lax.all_gather(factors, "grp", axis=1, tiled=True),
         lax.all_gather(tangent, "grp", axis=1, tiled=True),
     )
-    piece_u = lax.all_gather(group_u, "blk", axis=1, tiled=True)
-    piece_v = lax.all_gather(group_v, "blk", axis=1, tiled=True)
+    piece_u, piece_v = jnp.split(
+        lax.all_gather(jnp.concatenate([group_u, group_v], 0), "blk", axis=1, tiled=True),
+        [group_u.shape[0]],
+        0,
+    )
     width = piece_u.shape[1]
     eta = lax.dot_general(factors, piece_u, contract, precision=highest)
     deta = lax.dot_general(factors, piece_v, contract, precision=highest) + lax.dot_general(

time: 86.3 us -> 102 us (1.18)
  blocking collectives: 75 us -> 45 us
  waiting for transfers between devices: 0 us -> 29.2 us
  between operations: 0.69 us -> 14.1 us
  matrix products: 8.3 us -> 10.7 us
    all_gather x2 -> x0, blocking collectives: 32.6 us -> none  [the longest x1 16.6 us: local(): piece_u = lax.all_gather(group_u, 'blk', axis=1, tiled=True)]
    all_gather x0 -> x1, waiting for transfers between devices: none -> 29.2 us  [local(): lax.all_gather(jnp.concatenate([group_u, group_v], 0), 'blk', axis=1, til...]
    psum x1, blocking collectives: 30.1 us -> 32.6 us  [local(): lax.psum((jnp.sum(residual * residual), jnp.sum(tangent * hess_vec)), ('b...]
    dot_general x1, matrix products: 1.03 us -> 2.94 us  [local(): lax.dot_general(factors, piece_v, contract, precision=highest)]
    all_gather x1, blocking collectives: 5.58 us -> 6.82 us  [local(): lax.all_gather(tangent, 'grp', axis=1, tiled=True)]
    all_gather x1, blocking collectives: 6.69 us -> 5.58 us  [local(): lax.all_gather(factors, 'grp', axis=1, tiled=True)]
  transfers between devices with their start and end apart: 0 -> 1, of which waited for: 0 -> 1; matrix products, arithmetic and copies ran while one was open for 0% -> 0% of each run, Pallas kernels for 0% -> 0%
where the time goes in v1:
time: 102 us
  blocking collectives  45 us (44%)
  waiting for transfers between devices  29.2 us (29%)
  between operations  14.1 us (14%)
  matrix products  10.7 us (10%)
  other arithmetic  2.56 us (3%)
    psum x1, blocking collectives, local(): lax.psum((jnp.sum(residual * residual), jnp.sum(tangent * hess_vec)), ('b...  32.6 us
    all_gather x1, waiting for transfers between devices, local(): lax.all_gather(jnp.concatenate([group_u, group_v], 0), 'blk', axis=1, til...  29.2 us
    all_gather x1, blocking collectives, local(): lax.all_gather(tangent, 'grp', axis=1, tiled=True)  6.82 us
    all_gather x1, blocking collectives, local(): lax.all_gather(factors, 'grp', axis=1, tiled=True)  5.58 us
    dot_general x1, matrix products, local(): lax.dot_general(factors, piece_v, contract, precision=highest)  2.94 us
    dot_general x1, matrix products, local(): lax.dot_general(piece_u, slack - weight, right, precision=highest)  2.19 us
  transfers between devices with their start and end apart: 1, of which 1 were waited for; matrix products, arithmetic and copies ran while one was open for 0% of the time, Pallas kernels for 0%

profile of v1, /device:TPU:0, one launch (start us, length us, event | category | flops | bytes accessed | tf_op | source)
XLA Modules:
  0.0 102.0 jit_solution(14580952171395302995)
XLA Ops:
  7.2 0.0 copy-start.3
  7.2 0.0 copy-start.1
  7.2 0.0 all-gather.2.cloned.1.call-start
  7.2 6.8 %all_gather.10 = f32[64,512]{1,0:T(8,128)S(1)} all-gather(f32[64,128]{1,0:T(8,128)} %param.4), channel_id=1, replica_groups=mesh['parts'=2,'blk'=4,'grp'=4] {'grp'}, dimensions={1}, use_global_device_ids=true | all-gather | bytes 163840 | tf_op jit(solution)/shard_map/all_gather | solution.py:18
  14.1 0.0 copy-done.3
  14.1 5.6 %all_gather.9 = f32[64,512]{1,0:T(8,128)S(1)} all-gather(f32[64,128]{1,0:T(8,128)S(1)} %copy-done.3), channel_id=1, replica_groups=mesh['parts'=2,'blk'=4,'grp'=4] {'grp'}, dimensions={1}, use_global_device_ids=true | all-gather | bytes 163840 | tf_op jit(solution)/shard_map/all_gather | solution.py:17
  19.6 0.7 pad_maximum_fusion
  20.4 0.0 all-gather.2.cloned.1.call-update
  20.4 0.0 copy-done.1
  20.4 0.3 copy.6
  20.8 29.2 %all-gather.2.cloned.1.call-done = f32[128,2048]{1,0:T(8,128)} async-done(((f32[128,512]{1,0:T(8,128)}), f32[128,2048]{1,0:T(8,128)}) %all-gather.2.cloned.1.call-update) | async-done | bytes 1048592 | tf_op jit(solution)/shard_map/all_gather | solution.py:21
  50.0 0.0 copy-start
  50.0 2.9 %fusion.8 = f32[2048,128]{1,0:T(8,128)S(1)} fusion(f32[64,128]{1,0:T(8,128)S(1)} %copy-done.3, f32[128,2048]{1,0:T(8,128)} %all-gather.2.cloned.1.call-done), kind=kOutput, calls=%fused_computation.13 | convolution fusion | flops 201326592 | bytes 1605632 | tf_op jit(solution)/shard_map/dot_general | solution.py:27
  52.9 0.0 copy-done
  52.9 0.0 copy-start.2
  53.0 1.8 %fusion.3 = f32[128,2048]{0,1:T(8,128)S(1)} fusion(f32[64,128]{1,0:T(8,128)S(1)} %copy-done.3, s32[128]{0:T(128)S(1)} %iota_add_fusion, f32[128,2048]{1,0:T(8,128)S(1)} %copy-done), kind=kOutput, calls=%fused_computation.5 | convolution fusion | flops 201850880 | bytes 1606144 | tf_op jit(solution)/shard_map/dot_general | solution.py:26
  54.8 0.0 copy-done.2
  54.8 1.8 %fusion.1 = f32[128,2048]{0,1:T(8,128)S(1)} fusion(f32[128,2048]{0,1:T(8,128)S(1)} %fusion.3, f32[2048,128]{1,0:T(8,128)S(1)} %fusion.8, f32[64,128]{1,0:T(8,128)S(1)} %copy-done.2, f32[128,2048]{1,0:T(8,128)S(1)} %copy-done), kind=kOutput, calls=%fused_computation.2 | convolution fusion | flops 201850880 | bytes 3702784 | tf_op jit(solution)/shard_map/dot_general | solution.py:27
  56.6 2.0 %multiply_reduce_fusion = (f32[]{:T(128)}, f32[64,128]{1,0:T(8,128)}) fusion(f32[64,128]{1,0:T(8,128)S(1)} %copy-done.2, f32[128,2048]{0,1:T(8,128)S(1)} %fusion.1, f32[128,2048]{1,0:T(8,128)S(1)} %copy-done), kind=kOutput, calls=%fused_computation.22 | convolution fusion | flops 201351168 | bytes 1638404 | tf_op jit(solution)/shard_map/dot_general | solution.py:36
  58.6 2.2 %multiply_reduce_fusion.1 = (f32[]{:T(128)}, f32[64,128]{1,0:T(8,128)}) fusion(f32[128,2048]{0,1:T(8,128)S(1)} %fusion.1, f32[128,2048]{0,1:T(8,128)S(1)} %fusion.3, s32[128,2048]{0,1:T(8,128)S(1)} %copy.6, s32[128]{0:T(128)S(1)} %iota_add_fusion, f32[128,2048]{1,0:T(8,128)S(1)} %copy-done), kind=kOutput, calls=%fused_computation.23 | convolution fusion | flops 202661888 | bytes 3703300 | tf_op jit(solution)/shard_map/dot_general | solution.py:37
  60.7 32.6 %all-reduce = (f32[1]{0:T(128)}, f32[1]{0:T(128)}) all-reduce(f32[1]{0:T(128)} %bitcast.3, f32[1]{0:T(128)} %bitcast.2), channel_id=1, replica_groups=mesh['parts'=2,'blk'=4,'grp'=4] {'blk','grp'}, use_global_device_ids=true, to_apply=%region_3.4 | all-reduce | flops 2 | bytes 16 | tf_op jit(solution)/shard_map/psum | solution.py:41
  93.3 1.8 %pad_maximum_fusion.1 = f32[2]{0:T(128)} fusion(f32[1]{0:T(128)} %get-tuple-element.3, f32[1]{0:T(128)} %get-tuple-element.4), kind=kLoop, calls=%fused_computation.24 | loop fusion | flops 2 | bytes 16 | tf_op jit(solution)/shard_map/stack | solution.py:44
  (1 shorter events, 0.0 us)
Async XLA Ops:
  7.2 6.9 %copy-start.3 = (f32[64,128]{1,0:T(8,128)S(1)}, f32[64,128]{1,0:T(8,128)}, u32[]{:S(2)}) copy-start(f32[64,128]{1,0:T(8,128)} %param.3) | copy-start | bytes 98308
  7.2 13.2 %copy-start.1 = (s32[128,2048]{1,0:T(8,128)S(1)}, s32[128,2048]{1,0:T(8,128)}, u32[]{:S(2)}) copy-start(s32[128,2048]{1,0:T(8,128)} %param.5) | copy-start | bytes 3145732
  7.2 42.8 %all-gather.2.cloned.1.call-start = ((), (), s32[]{:S(2)}) async-start(), calls=%async_computation | async-start | bytes 1310720 | tf_op jit(solution)/shard_map/all_gather | solution.py:21
  50.0 3.0 %copy-start = (f32[128,2048]{1,0:T(8,128)S(1)}, f32[128,2048]{1,0:T(8,128)}, u32[]{:S(2)}) copy-start(f32[128,2048]{1,0:T(8,128)} %all-gather.2.cloned.1.call-done) | copy-start | bytes 3145732
  52.9 1.8 %copy-start.2 = (f32[64,128]{1,0:T(8,128)S(1)}, f32[64,128]{1,0:T(8,128)}, u32[]{:S(2)}) copy-start(f32[64,128]{1,0:T(8,128)} %param.4) | copy-start | bytes 98308
Sparse Core Ops, SparseCore 0:
  20.5 29.4 all-gather.1
